TPU v7x, 32 devices: a whole 2x2x4 slice. The times are simulated.
32 devices in a mesh: grp: 2 (over x), seq: 8 (over z, y), head: 2 (over core).
Axes of the slice: x: 2, y: 2, z: 4, core: 2. Of those that a mesh axis runs over, the one named last changes fastest.
Arguments:
- q_nope: bfloat16 [8, 128, 128], P('grp', ('seq', 'head')), parts along dimension 0, may hold values from -6 to 6
- q_rope: bfloat16 [8, 128, 64], P('grp', ('seq', 'head')), parts along dimension 0, may hold values from -150 to 150
- w_uk: bfloat16 [128, 128, 512], P(('seq', 'head')), may hold values from -0.5 to 0.5
- w_uv: bfloat16 [128, 512, 128], P(('seq', 'head')), may hold values from -1 to 1
- cache: bfloat16 [8, 4096, 576], P('grp', 'seq'), parts along dimension 0, may hold values from -12 to 12
- lengths: int32 [8], P('grp'), parts along dimension 0, may hold values from 2048 to 4096, as said below
- selected: int32 [8, 8, 32], P('grp'), parts along dimension 0, may hold values from 0 to 63, as said below
Outputs:
- attended: bfloat16 [8, 128, 128], P('grp', ('seq', 'head')), parts along dimension 0
- bounds: float32 [8, 8, 64], P('grp', None, 'seq'), parts along dimension 0
There are 2 independent parts, one for each index of `grp`. A program takes and returns all parts, laid end to end along the dimension named above; an argument that names none is the same for every part. Nothing has to cross between parts.
Inputs may be any that keep to these rules, and one draw needn't show every extreme that they name: `lengths`: some request has exactly 4096 cached tokens; every request has 2048 or more. `selected`: for each request and head group the 32 page numbers are distinct and below ceil(lengths[r] / 64); page 0 and the page of the request's last cached token are always among them.
All inputs are finite; a program needn't handle non-finite values.
Results may differ from a plain program's by a relative error of at most 0.0065.
Values may be sent and summed in bfloat16 or wider, within the bound.
A program may use at most 64 MiB of HBM per device.

v0:
```python
import jax
import jax.numpy as jnp
from jax import lax
from jax.sharding import PartitionSpec as P

GH = 16
PAGE = 64


def local(q_nope, q_rope, w_uk, w_uv, cache, lengths, selected):
    seq_count = lax.axis_size("seq")
    head_count = lax.axis_size("head")
    seq_rank = lax.axis_index("seq")
    head_rank = lax.axis_index("head")
    requests = q_nope.shape[0]
    head_block = q_nope.shape[1]
    latent_width = w_uk.shape[2]
    cache_width = cache.shape[2]
    tokens_here = cache.shape[1]
    pages_here = tokens_here // PAGE
    groups = selected.shape[1]
    softmax_scale = (q_nope.shape[2] + q_rope.shape[2]) ** (-0.5)
    query_latent = jnp.einsum(
        "rhn,hnl->rhl", q_nope, w_uk, preferred_element_type=jnp.float32
    ).astype(jnp.bfloat16)
    absorbed = jnp.concatenate([query_latent, q_rope], axis=2)
    queries = lax.all_gather(absorbed, "seq", axis=1, tiled=True)
    heads_here = head_block * seq_count
    position = jnp.arange(heads_here, dtype=jnp.int32)
    global_head = (
        position // head_block * head_count + head_rank
    ) * head_block + position % head_block
    group_of = global_head // GH
    group_hot = group_of[:, None] == jnp.arange(groups, dtype=jnp.int32)[None, :]
    page_number = seq_rank * pages_here + jnp.arange(pages_here, dtype=jnp.int32)
    token_index = seq_rank * tokens_here + jnp.arange(tokens_here, dtype=jnp.int32).reshape(
        pages_here, PAGE
    )
    live_token = token_index[None] < lengths[:, None, None]
    live_page = live_token[:, :, 0]
    page_blocks = cache.reshape(requests, pages_here, PAGE, cache_width)
    page_low = jnp.min(jnp.where(live_token[..., None], page_blocks, jnp.inf), axis=2).astype(
        jnp.float32
    )
    page_high = jnp.max(jnp.where(live_token[..., None], page_blocks, -jnp.inf), axis=2).astype(
        jnp.float32
    )
    page_low = jnp.where(live_page[..., None], page_low, 0.0)
    page_high = jnp.where(live_page[..., None], page_high, 0.0)
    middle = (page_low + page_high) * 0.5
    spread = (page_high - page_low) * 0.5
    query_float = queries.astype(jnp.float32)
    head_bound = softmax_scale * (
        jnp.einsum("rhd,rpd->rhp", query_float, middle, precision=lax.Precision.HIGHEST)
        + jnp.einsum("rhd,rpd->rhp", jnp.abs(query_float), spread, precision=lax.Precision.HIGHEST)
    )
    group_bound = jnp.max(
        jnp.where(group_hot.T[None, :, :, None], head_bound[:, None, :, :], -1e30), axis=2
    )
    group_bound = lax.pmax(group_bound, "head")
    bounds = jnp.where(live_page[:, None, :], group_bound, 0.0)
    picked = jnp.any(selected[:, :, :, None] == page_number[None, None, None, :], axis=2)
    head_pick = jnp.any(group_hot[None, :, :, None] & picked[:, None, :, :], axis=2)
    scores = (
        jnp.einsum("rhd,rtd->rht", queries, cache, preferred_element_type=jnp.float32)
        * softmax_scale
    )
    scores = scores.reshape(requests, heads_here, pages_here, PAGE)
    scores = jnp.where(live_token[:, None], scores, -1e30)
    page_top = jnp.max(scores, axis=3)
    weights = jnp.where(live_token[:, None], jnp.exp(scores - page_top[..., None]), 0.0).astype(
        jnp.bfloat16
    )
    page_total = jnp.sum(weights.astype(jnp.float32), axis=3)
    page_weighted = jnp.einsum(
        "rhpt,rptl->rhpl",
        weights,
        page_blocks[..., :latent_width],
        preferred_element_type=jnp.float32,
    )
    summit = jnp.max(jnp.where(head_pick, page_top, -1e30), axis=2)
    factor = jnp.where(head_pick, jnp.exp(page_top - summit[..., None]), 0.0)
    total = jnp.sum(factor * page_total, axis=2)
    weighted = jnp.einsum("rhp,rhpl->rhl", factor, page_weighted, precision=lax.Precision.HIGHEST)
    gotten = (
        lax.all_to_all(
            summit.reshape(requests, seq_count, head_block),
            "seq",
            split_axis=1,
            concat_axis=1,
            tiled=True,
        ),
        lax.all_to_all(
            total.reshape(requests, seq_count, head_block),
            "seq",
            split_axis=1,
            concat_axis=1,
            tiled=True,
        ),
        lax.all_to_all(
            weighted.reshape(requests, seq_count, head_block, latent_width),
            "seq",
            split_axis=1,
            concat_axis=1,
            tiled=True,
        ),
    )
    highest = jnp.max(gotten[0], axis=1)
    rescale = jnp.exp(gotten[0] - highest[:, None, :])
    own_total = jnp.sum(rescale * gotten[1], axis=1)
    own_weighted = jnp.sum(rescale[..., None] * gotten[2], axis=1)
    latent_out = (own_weighted / own_total[..., None]).astype(jnp.bfloat16)
    attended = jnp.einsum(
        "rhl,hlv->rhv", latent_out, w_uv, preferred_element_type=jnp.float32
    ).astype(jnp.bfloat16)
    return (attended, bounds)


def solution(mesh):
    placed = (
        P("grp", ("seq", "head"), None),
        P("grp", ("seq", "head"), None),
        P(("seq", "head"), None, None),
        P(("seq", "head"), None, None),
        P("grp", "seq", None),
        P("grp"),
        P("grp", None, None),
    )
    return jax.shard_map(
        local,
        mesh=mesh,
        in_specs=placed,
        out_specs=(P("grp", ("seq", "head"), None), P("grp", None, "seq")),
        check_vma=False,
    )
```

profile of v0, /device:TPU:0, one launch (start us, length us, event | category | flops | bytes accessed | tf_op | source)
XLA Modules:
  0.0 88.1 jit_solution(16813406923026156517)
XLA Ops:
  0.6 0.0 copy-start
  0.7 0.8 copy.102
  1.5 0.4 copy-done
  1.9 0.9 %fusion.3 = bf16[4,8,512]{2,0,1:T(4,128)(2,1)S(1)} fusion(bf16[8,128,512]{2,1,0:T(8,128)(2,1)S(1)} %copy-done, bf16[4,8,128]{2,1,0:T(8,128)(2,1)} %param.7), kind=kOutput, calls=%fused_computation.8 | convolution fusion | flops 4210688 | bytes 1089536 | tf_op jit(solution)/shard_map/rhn,hnl->rhl/dot_general | solution.py:23
  2.8 0.0 copy-start.3
  2.8 0.0 copy-start.4
  2.9 32.7 %all_gather.3 = bf16[4,64,576]{2,0,1:T(4,128)(2,1)S(1)} all-gather(bf16[4,8,576]{2,0,1:T(4,128)(2,1)S(1)} %pad_maximum_fusion), channel_id=1, replica_groups=mesh['grp'=2,'seq'=8,'head'=2] {'seq'}, dimensions={1}, use_global_device_ids=true | all-gather | bytes 331776 | tf_op jit(solution)/shard_map/all_gather | solution.py:27
  35.5 2.2 %convolution_multiply_fusion = f32[4,64,512]{2,1,0:T(8,128)S(1)} fusion(bf16[4,512,576]{1,2,0:T(8,128)(2,1)} %param.11, bf16[4,64,576]{2,0,1:T(4,128)(2,1)S(1)} %all_gather.3), kind=kOutput, calls=%fused_computation.6 | convolution fusion | flops 151126016 | bytes 3178496 | tf_op jit(solution)/shard_map/rhd,rtd->rht/dot_general | solution.py:65
  37.7 0.2 reshape.136
  37.9 0.0 copy-done.3
  38.0 0.7 compare_reduce_fusion
  38.6 0.1 and_reduce_fusion
  38.8 0.0 copy-done.4
  38.8 0.1 broadcast_compare_fusion
  38.9 0.4 fusion.6
  39.2 0.1 reshape.137
  39.3 0.6 copy.105
  39.9 5.6 %all-to-all-start = ((f32[4,8,8]{2,0,1:T(4,128)}), f32[4,8,8]{2,0,1:T(4,128)S(1)}, u32[]{:S(2)}, u32[]{:S(2)}) async-start(f32[4,8,8]{2,0,1:T(4,128)} %copy.105), calls=%async_computation | async-start | bytes 32768 | tf_op jit(solution)/shard_map/all_to_all | solution.py:86
  45.5 0.7 convert_reduce_fusion
  46.2 4.3 %copy.106 = bf16[4,512,576]{2,1,0:T(8,128)(2,1)} copy(bf16[4,512,576]{1,2,0:T(8,128)(2,1)} %param.11) | data formatting | bytes 4718592 | tf_op args[4]
  50.6 0.1 copy.114
  50.7 0.0 copy-start.1
  50.7 2.7 %select_reduce_fusion.1 = (bf16[4,8,576]{2,1,0:T(8,128)(2,1)S(1)}, bf16[4,8,576]{2,1,0:T(8,128)(2,1)S(1)}) fusion(pred[4,8,64]{2,1,0:T(8,128)(4,1)S(1)} %broadcast_compare_fusion, bf16[4,512,576]{2,1,0:T(8,128)(2,1)} %copy.106), kind=kLoop, calls=%fused_computation.3 | loop fusion | flops 4681728 | bytes 2435072 | tf_op jit(solution)/shard_map/reduce_min | solution.py:42
  53.4 0.0 copy-done.1
  53.4 1.0 %convolution_bitcast_fusion = f32[4,64,8,512]{3,1,2,0:T(8,128)S(1)} fusion(bf16[4,8,64,576]{3,2,1,0:T(8,128)(2,1)S(1)} %bitcast.20, f32[4,64,8,64]{3,2,1,0:T(8,128)S(1)} %reshape.136, f32[4,64,8]{1,2,0:T(8,128)S(1)} %fusion.6, pred[4,8,64]{2,1,0:T(8,128)(4,1)S(1)} %broadcast_compare_fusion), kind=kOutput, calls=%fused_computation.4 | convolution fusion | flops 134742016 | bytes 7360512 | tf_op jit(solution)/shard_map/rhpt,rptl->rhpl/dot_general | solution.py:75
  54.4 5.4 %fusion = f32[4,64,1,512]{3,2,1,0:T(1,128)S(1)} fusion(f32[4,64,8,1]{2,3,1,0:T(1,128)S(1)} %copy.114, f32[4,64,8,512]{3,1,2,0:T(8,128)S(1)} %convolution_bitcast_fusion), kind=kOutput, calls=%fused_computation | convolution fusion | flops 12582912 | bytes 4726784 | tf_op jit(solution)/shard_map/rhp,rhpl->rhl/dot_general | solution.py:84
  59.8 0.1 slice_reduce_fusion
  59.9 0.1 reshape.140
  60.0 0.6 copy.108
  60.6 0.0 all-to-all-done
  60.7 6.0 %all-to-all-start.2 = ((f32[4,8,8]{2,0,1:T(4,128)}), f32[4,8,8]{2,0,1:T(4,128)S(1)}, u32[]{:S(2)}, u32[]{:S(2)}) async-start(f32[4,8,8]{2,0,1:T(4,128)} %copy.108), calls=%async_computation.2 | async-start | bytes 32768 | tf_op jit(solution)/shard_map/all_to_all | solution.py:93
  66.7 0.0 copy-start.2
  66.7 0.5 fusion.10
  67.2 0.8 copy.107
  68.0 5.3 %all-to-all-done.2 = f32[4,8,8]{2,0,1:T(4,128)S(1)} async-done(((f32[4,8,8]{2,0,1:T(4,128)}), f32[4,8,8]{2,0,1:T(4,128)S(1)}, u32[]{:S(2)}, u32[]{:S(2)}) %all-to-all-start.2) | async-done | bytes 1056 | tf_op jit(solution)/shard_map/all_to_all | solution.py:93
  73.3 3.5 %all-to-all-start.1 = ((f32[4,8,8,512]{3,2,0,1:T(8,128)}), f32[4,8,8,512]{3,2,0,1:T(8,128)S(1)}, u32[]{:S(2)}, u32[]{:S(2)}) async-start(f32[4,8,8,512]{3,2,0,1:T(8,128)} %copy.107), calls=%async_computation.1 | async-start | bytes 1048576 | tf_op jit(solution)/shard_map/all_to_all | solution.py:100
  76.8 0.8 fusion.4
  77.6 0.1 select_reduce_fusion.2
  77.7 3.4 %pmax.7 = f32[4,8,8]{2,1,0:T(8,128)S(1)} all-reduce(f32[4,8,8]{2,1,0:T(8,128)S(1)} %select_reduce_fusion.2), channel_id=1, replica_groups=mesh['grp'=2,'seq'=8,'head'=2] {'head'}, use_global_device_ids=true, to_apply=%region_12.13 | all-reduce | flops 256 | bytes 2048 | tf_op jit(solution)/shard_map/pmax | solution.py:60
  81.1 0.6 broadcast_select_fusion
  81.8 5.2 %all-to-all-done.1 = f32[4,8,8,512]{3,2,0,1:T(8,128)S(1)} async-done(((f32[4,8,8,512]{3,2,0,1:T(8,128)}), f32[4,8,8,512]{3,2,0,1:T(8,128)S(1)}, u32[]{:S(2)}, u32[]{:S(2)}) %all-to-all-start.1) | async-done | bytes 524320 | tf_op jit(solution)/shard_map/all_to_all | solution.py:100
  87.0 0.1 multiply_reduce_fusion
  87.1 0.1 divide_convert_fusion
  87.2 0.0 copy-done.2
  87.2 0.2 fusion.5
  87.4 0.6 copy.113
  (11 shorter events, 0.2 us)
Async XLA Ops:
  0.6 1.2 %copy-start = (bf16[8,128,512]{2,1,0:T(8,128)(2,1)S(1)}, bf16[8,128,512]{2,1,0:T(8,128)(2,1)}, u32[]{:S(2)}) copy-start(bf16[8,128,512]{2,1,0:T(8,128)(2,1)} %param.9) | copy-start | bytes 3145732
  2.8 35.1 %copy-start.3 = (s32[4,8,32]{2,1,0:T(8,128)S(1)}, s32[4,8,32]{2,1,0:T(8,128)}, u32[]{:S(2)}) copy-start(s32[4,8,32]{2,1,0:T(8,128)} %param.13) | copy-start | bytes 12292
  2.8 36.0 %copy-start.4 = (s32[4]{0:T(128)S(1)}, s32[4]{0:T(128)}, u32[]{:S(2)}) copy-start(s32[4]{0:T(128)} %param.12) | copy-start | bytes 52
  39.9 20.7 %all-to-all-start = ((f32[4,8,8]{2,0,1:T(4,128)}), f32[4,8,8]{2,0,1:T(4,128)S(1)}, u32[]{:S(2)}, u32[]{:S(2)}) async-start(f32[4,8,8]{2,0,1:T(4,128)} %copy.105), calls=%async_computation | async-start | bytes 32768 | tf_op jit(solution)/shard_map/all_to_all | solution.py:86
  50.7 2.7 %copy-start.1 = (bf16[4,512,576]{2,1,0:T(8,128)(2,1)S(1)}, bf16[4,512,576]{2,1,0:T(8,128)(2,1)}, u32[]{:S(2)}) copy-start(bf16[4,512,576]{2,1,0:T(8,128)(2,1)} %copy.106) | copy-start | bytes 7077892
  60.7 12.6 %all-to-all-start.2 = ((f32[4,8,8]{2,0,1:T(4,128)}), f32[4,8,8]{2,0,1:T(4,128)S(1)}, u32[]{:S(2)}, u32[]{:S(2)}) async-start(f32[4,8,8]{2,0,1:T(4,128)} %copy.108), calls=%async_computation.2 | async-start | bytes 32768 | tf_op jit(solution)/shard_map/all_to_all | solution.py:93
  66.7 20.5 %copy-start.2 = (bf16[8,512,128]{2,1,0:T(8,128)(2,1)S(1)}, bf16[8,512,128]{2,1,0:T(8,128)(2,1)}, u32[]{:S(2)}) copy-start(bf16[8,512,128]{2,1,0:T(8,128)(2,1)} %param.10) | copy-start | bytes 3145732
  73.3 13.7 %all-to-all-start.1 = ((f32[4,8,8,512]{3,2,0,1:T(8,128)}), f32[4,8,8,512]{3,2,0,1:T(8,128)S(1)}, u32[]{:S(2)}, u32[]{:S(2)}) async-start(f32[4,8,8,512]{3,2,0,1:T(8,128)} %copy.107), calls=%async_computation.1 | async-start | bytes 1048576 | tf_op jit(solution)/shard_map/all_to_all | solution.py:100
where the time goes:
time: 88.6 us; the launch traced here: 88.1 us
  blocking collectives  36 us (41%)
  starting transfers between devices  15.1 us (17%)
  matrix products  11 us (12%)
  waiting for transfers between devices  10.5 us (12%)
  local copies, waits for them, and re-layouts  8.85 us (10%)
  other arithmetic  5.68 us (6%)
    all_gather x1, blocking collectives, local(): queries = lax.all_gather(absorbed, 'seq', axis=1, tiled=True)  32.7 us
    unnamed x13, local copies, waits for them, and re-layouts  6.15 us
    all_to_all x1, starting transfers between devices, local(): lax.all_to_all(total.reshape(requests, seq_count, head_block), 'seq', spl...  6.01 us
    all_to_all x1, starting transfers between devices, local(): lax.all_to_all(summit.reshape(requests, seq_count, head_block), 'seq', sp...  5.61 us
    dot_general x1, matrix products, local(): jnp.einsum('rhp,rhpl->rhl', factor, page_weighted, precision=lax.Precisio...  5.37 us
    all_to_all x1, waiting for transfers between devices, local(): lax.all_to_all(total.reshape(requests, seq_count, head_block), 'seq', spl...  5.28 us
    all_to_all x1, waiting for transfers between devices, local(): lax.all_to_all(weighted.reshape(requests, seq_count, head_block, latent_w...  5.23 us
    all_to_all x1, starting transfers between devices, local(): lax.all_to_all(weighted.reshape(requests, seq_count, head_block, latent_w...  3.49 us
  transfers between devices with their start and end apart: 3, of which 2 were waited for; matrix products, arithmetic and copies ran while one was open for 20% of the time, Pallas kernels for 0%

commit v1 on v0

--- a/solution.py
+++ b/solution.py
@@ -2,6 +2,7 @@
 import jax.numpy as jnp
 from jax import lax
 from jax.sharding import PartitionSpec as P
+from jax.lax import axis_index, axis_size, ppermute
 
 GH = 16
 PAGE = 64
@@ -24,7 +25,21 @@
         "rhn,hnl->rhl", q_nope, w_uk, preferred_element_type=jnp.float32
     ).astype(jnp.bfloat16)
     absorbed = jnp.concatenate([query_latent, q_rope], axis=2)
-    queries = lax.all_gather(absorbed, "seq", axis=1, tiled=True)
+    mat = absorbed
+    heard, row_out, far_arr = (axis_size("seq"), axis_index("seq"), mat.shape[1])
+    seen = [hop_no * heard if tick == 1 else hop_no for tick, hop_no in enumerate(mat.shape)]
+    queries = lax.dynamic_update_slice_in_dim(
+        jnp.zeros(seen, mat.dtype), mat, row_out * far_arr, axis=1
+    )
+    h = 1
+    while h < heard:
+        mat = ppermute(
+            mat, axis_name="seq", perm=[(tick, (tick + 1) % heard) for tick in range(heard)]
+        )
+        queries = lax.dynamic_update_slice_in_dim(
+            queries, mat, (row_out - h) % heard * far_arr, axis=1
+        )
+        h += 1
     heads_here = head_block * seq_count
     position = jnp.arange(heads_here, dtype=jnp.int32)
     global_head = (

time: 88.6 us -> 105 us (1.19)
  blocking collectives: 36 us -> 3.36 us
  waiting for transfers between devices: 10.5 us -> 39.3 us
  matrix products: 11 us -> 19.2 us
  local copies, waits for them, and re-layouts: 8.85 us -> 15.7 us
  starting transfers between devices: 15.1 us -> 18.5 us
  other arithmetic: 5.68 us -> 7.2 us
    ppermute x0 -> x7, waiting for transfers between devices: none -> 34.9 us  [local(): ppermute(mat, axis_name='seq', perm=[(tick, (tick + 1) % heard) for tick...]
    all_gather x1 -> x0, blocking collectives: 32.7 us -> none  [local(): queries = lax.all_gather(absorbed, 'seq', axis=1, tiled=True)]
    dynamic_update_slice x0 -> x8, local copies, waits for them, and re-layouts: none -> 5.02 us  [the longest x7 4.4 us: local(): lax.dynamic_update_slice_in_dim(queries, mat, (row_out - h) % heard * far...]
    ppermute x0 -> x7, starting transfers between devices: none -> 4.63 us  [local(): ppermute(mat, axis_name='seq', perm=[(tick, (tick + 1) % heard) for tick...]
    all_to_all x1, waiting for transfers between devices: 5.28 us -> 1.46 us  [local(): lax.all_to_all(total.reshape(requests, seq_count, head_block), 'seq', spl...]
    dot_general x1, matrix products: 1.03 us -> 4.28 us  [local(): jnp.einsum('rhpt,rptl->rhpl', weights, page_blocks[..., :latent_width], p...]
    dot_general x1, matrix products: 5.37 us -> 8.21 us  [local(): jnp.einsum('rhp,rhpl->rhl', factor, page_weighted, precision=lax.Precisio...]
    all_to_all x1, starting transfers between devices: 6.01 us -> 3.34 us  [local(): lax.all_to_all(total.reshape(requests, seq_count, head_block), 'seq', spl...]
  transfers between devices with their start and end apart: 3 -> 10, of which waited for: 2 -> 8; matrix products, arithmetic and copies ran while one was open for 20% -> 32% of each run, Pallas kernels for 0% -> 0%
where the time goes in v1:
time: 105 us; the launch traced here: 104 us
  waiting for transfers between devices  39.3 us (37%)
  matrix products  19.2 us (18%)
  starting transfers between devices  18.5 us (18%)
  local copies, waits for them, and re-layouts  15.7 us (15%)
  other arithmetic  7.2 us (7%)
  blocking collectives  3.36 us (3%)
    ppermute x7, waiting for transfers between devices, local(): ppermute(mat, axis_name='seq', perm=[(tick, (tick + 1) % heard) for tick...  34.9 us
    dot_general x1, matrix products, local(): jnp.einsum('rhp,rhpl->rhl', factor, page_weighted, precision=lax.Precisio...  8.21 us
    unnamed x19, local copies, waits for them, and re-layouts  6.25 us
    all_to_all x1, starting transfers between devices, local(): lax.all_to_all(weighted.reshape(requests, seq_count, head_block, latent_w...  6 us
    ppermute x7, starting transfers between devices, local(): ppermute(mat, axis_name='seq', perm=[(tick, (tick + 1) % heard) for tick...  4.63 us
    all_to_all x1, starting transfers between devices, local(): lax.all_to_all(summit.reshape(requests, seq_count, head_block), 'seq', sp...  4.52 us
    dynamic_update_slice x7, local copies, waits for them, and re-layouts, local(): lax.dynamic_update_slice_in_dim(queries, mat, (row_out - h) % heard * far...  4.4 us
    dot_general x1, matrix products, local(): jnp.einsum('rhpt,rptl->rhpl', weights, page_blocks[..., :latent_width], p...  4.28 us
  transfers between devices with their start and end apart: 10, of which 8 were waited for; matrix products, arithmetic and copies ran while one was open for 32% of the time, Pallas kernels for 0%

profile of v1, /device:TPU:0, one launch (start us, length us, event | category | flops | bytes accessed | tf_op | source)
XLA Modules:
  0.0 104.2 jit_solution(5016037063882922585)
XLA Ops:
  0.6 0.0 copy-start
  0.6 0.8 copy.137
  1.4 0.4 copy-done
  1.9 0.9 fusion.3
  2.9 3.0 %collective-permute-start = (bf16[4,8,576]{2,0,1:T(4,128)(2,1)S(1)}, bf16[4,8,576]{2,0,1:T(4,128)(2,1)S(1)}, u32[]{:S(2)}, u32[]{:S(2)}) collective-permute-start(bf16[4,8,576]{2,0,1:T(4,128)(2,1)S(1)} %pad_maximum_fusion), channel_id=1, source_target_pairs={{0,2},{2,4},{4,6},{6,8},{8,10},{10,12},{12,14},{14,0},{1,3},{3,5},... | collective-permute-start | bytes 110600 | tf_op jit(solution)/shard_map/ppermute | solution.py:36
  5.9 0.6 iota_compare_fusion.1
  6.5 0.5 iota_add_fusion
  7.0 4.4 %copy.148 = bf16[4,512,576]{2,1,0:T(8,128)(2,1)} copy(bf16[4,512,576]{1,2,0:T(8,128)(2,1)} %param.11) | data formatting | bytes 4718592 | tf_op args[4]
  11.4 0.8 broadcast_in_dim.116
  12.2 0.6 copy_dynamic-update-slice_fusion.7
  12.8 0.1 broadcast_compare_fusion
  12.9 3.1 %select_reduce_fusion.1 = (bf16[4,8,576]{2,1,0:T(8,128)(2,1)S(1)}, bf16[4,8,576]{2,1,0:T(8,128)(2,1)}) fusion(pred[4,8,64]{2,1,0:T(8,128)(4,1)S(1)} %broadcast_compare_fusion, bf16[4,512,576]{2,1,0:T(8,128)(2,1)} %copy.148), kind=kLoop, calls=%fused_computation.3 | loop fusion | flops 4681728 | bytes 2435072 | tf_op jit(solution)/shard_map/reduce_min | solution.py:57
  16.0 0.7 compare_reduce_fusion
  16.7 0.0 copy-done.5
  16.7 0.1 and_reduce_fusion
  16.8 0.1 slice_reduce_fusion
  17.1 0.0 collective-permute-done
  17.1 1.6 %collective-permute-start.1 = (bf16[4,8,576]{2,0,1:T(4,128)(2,1)S(1)}, bf16[4,8,576]{2,0,1:T(4,128)(2,1)S(1)}, u32[]{:S(2)}, u32[]{:S(2)}) collective-permute-start(bf16[4,8,576]{2,0,1:T(4,128)(2,1)S(1)} %collective-permute-done), channel_id=1, source_target_pairs={{0,2},{2,4},{4,6},{6,8},{8,10},{10,12},{12,14},{14,0},{1,3},{3,5},... | collective-permute-start | bytes 110600 | tf_op jit(solution)/shard_map/ppermute | solution.py:36
  18.7 0.6 copy_dynamic-update-slice_fusion.6
  19.3 4.6 %collective-permute-done.1 = bf16[4,8,576]{2,0,1:T(4,128)(2,1)S(1)} collective-permute-done((bf16[4,8,576]{2,0,1:T(4,128)(2,1)S(1)}, bf16[4,8,576]{2,0,1:T(4,128)(2,1)S(1)}, u32[]{:S(2)}, u32[]{:S(2)}) %collective-permute-start.1) | collective-permute-done | bytes 36896 | tf_op jit(solution)/shard_map/ppermute | solution.py:36
  23.9 0.0 collective-permute-start.2
  23.9 0.6 copy_dynamic-update-slice_fusion.5
  24.5 6.1 %collective-permute-done.2 = bf16[4,8,576]{2,0,1:T(4,128)(2,1)S(1)} collective-permute-done((bf16[4,8,576]{2,0,1:T(4,128)(2,1)S(1)}, bf16[4,8,576]{2,0,1:T(4,128)(2,1)S(1)}, u32[]{:S(2)}, u32[]{:S(2)}) %collective-permute-start.2) | collective-permute-done | bytes 36896 | tf_op jit(solution)/shard_map/ppermute | solution.py:36
  30.6 0.0 collective-permute-start.3
  30.6 0.6 copy_dynamic-update-slice_fusion.4
  31.2 6.1 %collective-permute-done.3 = bf16[4,8,576]{2,0,1:T(4,128)(2,1)S(1)} collective-permute-done((bf16[4,8,576]{2,0,1:T(4,128)(2,1)S(1)}, bf16[4,8,576]{2,0,1:T(4,128)(2,1)S(1)}, u32[]{:S(2)}, u32[]{:S(2)}) %collective-permute-start.3) | collective-permute-done | bytes 36896 | tf_op jit(solution)/shard_map/ppermute | solution.py:36
  37.3 0.0 collective-permute-start.4
  37.3 0.6 copy_dynamic-update-slice_fusion.3
  37.9 6.1 %collective-permute-done.4 = bf16[4,8,576]{2,0,1:T(4,128)(2,1)S(1)} collective-permute-done((bf16[4,8,576]{2,0,1:T(4,128)(2,1)S(1)}, bf16[4,8,576]{2,0,1:T(4,128)(2,1)S(1)}, u32[]{:S(2)}, u32[]{:S(2)}) %collective-permute-start.4) | collective-permute-done | bytes 36896 | tf_op jit(solution)/shard_map/ppermute | solution.py:36
  44.0 0.0 collective-permute-start.5
  44.0 0.6 copy_dynamic-update-slice_fusion.2
  44.6 6.1 %collective-permute-done.5 = bf16[4,8,576]{2,0,1:T(4,128)(2,1)S(1)} collective-permute-done((bf16[4,8,576]{2,0,1:T(4,128)(2,1)S(1)}, bf16[4,8,576]{2,0,1:T(4,128)(2,1)S(1)}, u32[]{:S(2)}, u32[]{:S(2)}) %collective-permute-start.5) | collective-permute-done | bytes 36896 | tf_op jit(solution)/shard_map/ppermute | solution.py:36
  50.7 0.0 collective-permute-start.6
  50.7 0.6 copy_dynamic-update-slice_fusion.1
  51.3 6.1 %collective-permute-done.6 = bf16[4,8,576]{2,0,1:T(4,128)(2,1)S(1)} collective-permute-done((bf16[4,8,576]{2,0,1:T(4,128)(2,1)S(1)}, bf16[4,8,576]{2,0,1:T(4,128)(2,1)S(1)}, u32[]{:S(2)}, u32[]{:S(2)}) %collective-permute-start.6) | collective-permute-done | bytes 36896 | tf_op jit(solution)/shard_map/ppermute | solution.py:36
  57.4 0.6 copy_dynamic-update-slice_fusion
  58.0 2.3 %convolution_multiply_fusion = f32[4,64,512]{2,1,0:T(8,128)} fusion(bf16[4,64,576]{2,1,0:T(8,128)(2,1)} %copy_dynamic-update-slice_fusion, bf16[4,512,576]{1,2,0:T(8,128)(2,1)S(1)} %copy-done.1), kind=kOutput, calls=%fused_computation.6 | convolution fusion | flops 151126016 | bytes 3178496 | tf_op jit(solution)/shard_map/rhd,rtd->rht/dot_general | solution.py:80
  60.3 1.2 %reshape.136 = f32[4,64,8,64]{3,2,1,0:T(8,128)S(1)} reshape(f32[4,64,512]{2,1,0:T(8,128)} %convolution_multiply_fusion) | data formatting | bytes 1048576 | tf_op jit(solution)/shard_map/reshape | solution.py:83
  61.5 0.4 fusion.6
  61.9 0.7 convert_reduce_fusion
  62.6 0.1 reshape.140
  62.7 0.6 copy.150
  63.3 3.3 %all-to-all-start.2 = ((f32[4,8,8]{2,0,1:T(4,128)}), f32[4,8,8]{2,0,1:T(4,128)S(1)}, u32[]{:S(2)}, u32[]{:S(2)}) async-start(f32[4,8,8]{2,0,1:T(4,128)} %copy.150), calls=%async_computation.2 | async-start | bytes 32768 | tf_op jit(solution)/shard_map/all_to_all | solution.py:108
  66.7 4.3 %convolution_bitcast_fusion = f32[4,64,8,512]{3,1,2,0:T(8,128)} fusion(bf16[4,8,64,576]{3,2,1,0:T(8,128)(2,1)} %bitcast.22, f32[4,64,8,64]{3,2,1,0:T(8,128)S(1)} %reshape.136, f32[4,64,8]{1,2,0:T(8,128)S(1)} %fusion.6, pred[4,8,64]{2,1,0:T(8,128)(4,1)S(1)} %broadcast_compare_fusion), kind=kOutput, calls=%fused_computation.4 | convolution fusion | flops 134742016 | bytes 6825984 | tf_op jit(solution)/shard_map/rhpt,rptl->rhpl/dot_general | solution.py:90
  71.0 0.1 reshape.137
  71.0 0.6 copy.147
  71.6 0.1 copy.154
  71.7 1.5 %all-to-all-done.2 = f32[4,8,8]{2,0,1:T(4,128)S(1)} async-done(((f32[4,8,8]{2,0,1:T(4,128)}), f32[4,8,8]{2,0,1:T(4,128)S(1)}, u32[]{:S(2)}, u32[]{:S(2)}) %all-to-all-start.2) | async-done | bytes 1056 | tf_op jit(solution)/shard_map/all_to_all | solution.py:108
  73.2 4.5 %all-to-all-start = ((f32[4,8,8]{2,0,1:T(4,128)}), f32[4,8,8]{2,0,1:T(4,128)S(1)}, u32[]{:S(2)}, u32[]{:S(2)}) async-start(f32[4,8,8]{2,0,1:T(4,128)} %copy.147), calls=%async_computation | async-start | bytes 32768 | tf_op jit(solution)/shard_map/all_to_all | solution.py:101
  77.7 8.2 %fusion = f32[4,64,1,512]{3,2,1,0:T(1,128)S(1)} fusion(f32[4,64,8,1]{2,3,1,0:T(1,128)S(1)} %copy.154, f32[4,64,8,512]{3,1,2,0:T(8,128)} %convolution_bitcast_fusion), kind=kOutput, calls=%fused_computation | convolution fusion | flops 12582912 | bytes 4726784 | tf_op jit(solution)/shard_map/rhp,rhpl->rhl/dot_general | solution.py:99
  85.9 0.0 copy-start.2
  86.0 0.8 copy.149
  86.8 0.0 all-to-all-done
  86.8 6.0 %all-to-all-start.1 = ((f32[4,8,8,512]{3,2,0,1:T(8,128)}), f32[4,8,8,512]{3,2,0,1:T(8,128)S(1)}, u32[]{:S(2)}, u32[]{:S(2)}) async-start(f32[4,8,8,512]{3,2,0,1:T(8,128)} %copy.149), calls=%async_computation.1 | async-start | bytes 1048576 | tf_op jit(solution)/shard_map/all_to_all | solution.py:115
  92.8 1.8 %fusion.7 = f32[4,64,8]{1,2,0:T(8,128)S(1)} fusion(bf16[4,64,576]{2,1,0:T(8,128)(2,1)} %copy_dynamic-update-slice_fusion, bf16[4,8,576]{2,1,0:T(8,128)(2,1)S(1)} %copy-done.3, bf16[4,8,576]{2,1,0:T(8,128)(2,1)S(1)} %get-tuple-element.18, pred[4,8]{1,0:T(4,128)(4,1)S(1)} %slice_reduce_fusion), kind=kOutput, calls=%fused_computation.17 | convolution fusion | flops 14561280 | bytes 376864 | tf_op jit(solution)/shard_map/rhd,rpd->rhp/dot_general | solution.py:70
  94.6 1.5 %fusion.4 = f32[4,64,8]{1,2,0:T(8,128)S(1)} fusion(f32[4,64,8]{1,2,0:T(8,128)S(1)} %fusion.7, bf16[4,64,576]{2,1,0:T(8,128)(2,1)} %copy_dynamic-update-slice_fusion, bf16[4,8,576]{2,1,0:T(8,128)(2,1)S(1)} %copy-done.3, bf16[4,8,576]{2,1,0:T(8,128)(2,1)S(1)} %get-tuple-element.18, pred[4,8]{1,0:T(4,128)(4,1)S(1)} %slice_reduce_fusion), kind=kOutput, calls=%fused_computation.10 | convolution fusion | flops 14270464 | bytes 385056 | tf_op jit(solution)/shard_map/rhd,rpd->rhp/dot_general | solution.py:69
  96.0 0.1 select_reduce_fusion.2
  96.2 3.4 %pmax.7 = f32[4,8,8]{2,1,0:T(8,128)S(1)} all-reduce(f32[4,8,8]{2,1,0:T(8,128)S(1)} %select_reduce_fusion.2), channel_id=1, replica_groups=mesh['grp'=2,'seq'=8,'head'=2] {'head'}, use_global_device_ids=true, to_apply=%region_12.13 | all-reduce | flops 256 | bytes 2048 | tf_op jit(solution)/shard_map/pmax | solution.py:75
  99.5 0.6 broadcast_select_fusion
  100.2 2.9 %all-to-all-done.1 = f32[4,8,8,512]{3,2,0,1:T(8,128)S(1)} async-done(((f32[4,8,8,512]{3,2,0,1:T(8,128)}), f32[4,8,8,512]{3,2,0,1:T(8,128)S(1)}, u32[]{:S(2)}, u32[]{:S(2)}) %all-to-all-start.1) | async-done | bytes 524320 | tf_op jit(solution)/shard_map/all_to_all | solution.py:115
  103.1 0.1 multiply_reduce_fusion
  103.2 0.1 divide_convert_fusion
  103.3 0.2 fusion.5
  103.6 0.6 copy.153
  (21 shorter events, 0.2 us)
Async XLA Ops:
  0.6 1.2 %copy-start = (bf16[8,128,512]{2,1,0:T(8,128)(2,1)S(1)}, bf16[8,128,512]{2,1,0:T(8,128)(2,1)}, u32[]{:S(2)}) copy-start(bf16[8,128,512]{2,1,0:T(8,128)(2,1)} %param.9) | copy-start | bytes 3145732
  2.9 14.3 %collective-permute-start = (bf16[4,8,576]{2,0,1:T(4,128)(2,1)S(1)}, bf16[4,8,576]{2,0,1:T(4,128)(2,1)S(1)}, u32[]{:S(2)}, u32[]{:S(2)}) collective-permute-start(bf16[4,8,576]{2,0,1:T(4,128)(2,1)S(1)} %pad_maximum_fusion), channel_id=1, source_target_pairs={{0,2},{2,4},{4,6},{6,8},{8,10},{10,12},{12,14},{14,0},{1,3},{3,5},... | collective-permute-start | bytes 110600 | tf_op jit(solution)/shard_map/ppermute | solution.py:36
  7.0 5.8 %copy-start.6 = (s32[4]{0:T(128)S(1)}, s32[4]{0:T(128)}, u32[]{:S(2)}) copy-start(s32[4]{0:T(128)} %param.12) | copy-start | bytes 52
  11.4 4.6 %copy-start.4 = (s32[4,8,32]{2,1,0:T(8,128)S(1)}, s32[4,8,32]{2,1,0:T(8,128)}, u32[]{:S(2)}) copy-start(s32[4,8,32]{2,1,0:T(8,128)} %param.13) | copy-start | bytes 12292
  11.4 46.6 %copy-start.1 = (bf16[4,512,576]{1,2,0:T(8,128)(2,1)S(1)}, bf16[4,512,576]{1,2,0:T(8,128)(2,1)}, u32[]{:S(2)}) copy-start(bf16[4,512,576]{1,2,0:T(8,128)(2,1)} %param.11) | copy-start | bytes 7077892
  11.4 4.6 %copy-start.7 = (s32[8]{0:T(128)S(1)}, s32[8]{0:T(128)}, u32[]{:S(2)}) copy-start(s32[8]{0:T(128)} %iota_add_fusion) | copy-start | bytes 100
  11.4 5.3 %copy-start.5 = (pred[64,8]{0,1:T(8,128)(4,1)S(1)}, pred[64,8]{0,1:T(8,128)(4,1)}, u32[]{:S(2)}) copy-start(pred[64,8]{0,1:T(8,128)(4,1)} %iota_compare_fusion.1) | copy-start | bytes 1540
  17.1 6.8 %collective-permute-start.1 = (bf16[4,8,576]{2,0,1:T(4,128)(2,1)S(1)}, bf16[4,8,576]{2,0,1:T(4,128)(2,1)S(1)}, u32[]{:S(2)}, u32[]{:S(2)}) collective-permute-start(bf16[4,8,576]{2,0,1:T(4,128)(2,1)S(1)} %collective-permute-done), channel_id=1, source_target_pairs={{0,2},{2,4},{4,6},{6,8},{8,10},{10,12},{12,14},{14,0},{1,3},{3,5},... | collective-permute-start | bytes 110600 | tf_op jit(solution)/shard_map/ppermute | solution.py:36
  23.9 6.7 %collective-permute-start.2 = (bf16[4,8,576]{2,0,1:T(4,128)(2,1)S(1)}, bf16[4,8,576]{2,0,1:T(4,128)(2,1)S(1)}, u32[]{:S(2)}, u32[]{:S(2)}) collective-permute-start(bf16[4,8,576]{2,0,1:T(4,128)(2,1)S(1)} %collective-permute-done.1), channel_id=1, source_target_pairs={{0,2},{2,4},{4,6},{6,8},{8,10},{10,12},{12,14},{14,0},{1,3},{3,5},... | collective-permute-start | bytes 110600 | tf_op jit(solution)/shard_map/ppermute | solution.py:36
  30.6 6.7 %collective-permute-start.3 = (bf16[4,8,576]{2,0,1:T(4,128)(2,1)S(1)}, bf16[4,8,576]{2,0,1:T(4,128)(2,1)S(1)}, u32[]{:S(2)}, u32[]{:S(2)}) collective-permute-start(bf16[4,8,576]{2,0,1:T(4,128)(2,1)S(1)} %collective-permute-done.2), channel_id=1, source_target_pairs={{0,2},{2,4},{4,6},{6,8},{8,10},{10,12},{12,14},{14,0},{1,3},{3,5},... | collective-permute-start | bytes 110600 | tf_op jit(solution)/shard_map/ppermute | solution.py:36
  37.3 6.7 %collective-permute-start.4 = (bf16[4,8,576]{2,0,1:T(4,128)(2,1)S(1)}, bf16[4,8,576]{2,0,1:T(4,128)(2,1)S(1)}, u32[]{:S(2)}, u32[]{:S(2)}) collective-permute-start(bf16[4,8,576]{2,0,1:T(4,128)(2,1)S(1)} %collective-permute-done.3), channel_id=1, source_target_pairs={{0,2},{2,4},{4,6},{6,8},{8,10},{10,12},{12,14},{14,0},{1,3},{3,5},... | collective-permute-start | bytes 110600 | tf_op jit(solution)/shard_map/ppermute | solution.py:36
  44.0 6.7 %collective-permute-start.5 = (bf16[4,8,576]{2,0,1:T(4,128)(2,1)S(1)}, bf16[4,8,576]{2,0,1:T(4,128)(2,1)S(1)}, u32[]{:S(2)}, u32[]{:S(2)}) collective-permute-start(bf16[4,8,576]{2,0,1:T(4,128)(2,1)S(1)} %collective-permute-done.4), channel_id=1, source_target_pairs={{0,2},{2,4},{4,6},{6,8},{8,10},{10,12},{12,14},{14,0},{1,3},{3,5},... | collective-permute-start | bytes 110600 | tf_op jit(solution)/shard_map/ppermute | solution.py:36
  50.7 6.7 %collective-permute-start.6 = (bf16[4,8,576]{2,0,1:T(4,128)(2,1)S(1)}, bf16[4,8,576]{2,0,1:T(4,128)(2,1)S(1)}, u32[]{:S(2)}, u32[]{:S(2)}) collective-permute-start(bf16[4,8,576]{2,0,1:T(4,128)(2,1)S(1)} %collective-permute-done.5), channel_id=1, source_target_pairs={{0,2},{2,4},{4,6},{6,8},{8,10},{10,12},{12,14},{14,0},{1,3},{3,5},... | collective-permute-start | bytes 110600 | tf_op jit(solution)/shard_map/ppermute | solution.py:36
  63.3 9.9 %all-to-all-start.2 = ((f32[4,8,8]{2,0,1:T(4,128)}), f32[4,8,8]{2,0,1:T(4,128)S(1)}, u32[]{:S(2)}, u32[]{:S(2)}) async-start(f32[4,8,8]{2,0,1:T(4,128)} %copy.150), calls=%async_computation.2 | async-start | bytes 32768 | tf_op jit(solution)/shard_map/all_to_all | solution.py:108
  73.2 13.6 %all-to-all-start = ((f32[4,8,8]{2,0,1:T(4,128)}), f32[4,8,8]{2,0,1:T(4,128)S(1)}, u32[]{:S(2)}, u32[]{:S(2)}) async-start(f32[4,8,8]{2,0,1:T(4,128)} %copy.147), calls=%async_computation | async-start | bytes 32768 | tf_op jit(solution)/shard_map/all_to_all | solution.py:101
  85.9 6.9 %copy-start.3 = (bf16[4,8,576]{2,1,0:T(8,128)(2,1)S(1)}, bf16[4,8,576]{2,1,0:T(8,128)(2,1)}, u32[]{:S(2)}) copy-start(bf16[4,8,576]{2,1,0:T(8,128)(2,1)} %get-tuple-element.19) | copy-start | bytes 110596
  85.9 17.4 %copy-start.2 = (bf16[8,512,128]{2,1,0:T(8,128)(2,1)S(1)}, bf16[8,512,128]{2,1,0:T(8,128)(2,1)}, u32[]{:S(2)}) copy-start(bf16[8,512,128]{2,1,0:T(8,128)(2,1)} %param.10) | copy-start | bytes 3145732
  86.8 16.3 %all-to-all-start.1 = ((f32[4,8,8,512]{3,2,0,1:T(8,128)}), f32[4,8,8,512]{3,2,0,1:T(8,128)S(1)}, u32[]{:S(2)}, u32[]{:S(2)}) async-start(f32[4,8,8,512]{3,2,0,1:T(8,128)} %copy.149), calls=%async_computation.1 | async-start | bytes 1048576 | tf_op jit(solution)/shard_map/all_to_all | solution.py:115
